TPU v7x, 32 devices: a whole 2x2x4 slice. The times are simulated.
32 devices in a mesh: edata: 4 (over z), expert: 8 (over y, x, core).
Axes of the slice: x: 2, y: 2, z: 4, core: 2. Of those that a mesh axis runs over, the one named last changes fastest.
Arguments:
- tokens: bfloat16 [1024, 4096], P('expert', 'edata'), may hold values from -6 to 6
- grad_out: bfloat16 [1024, 4096], P('expert', 'edata'), may hold values from -6 to 6
- expert_ids: int32 [1024, 8], P('expert'), may hold values from 0 to 15, all different within a row; in each aligned block of 128 rows (0 to 127, 128 to 255, ...) at most 80 rows name the same one
- route_prob: float32 [1024, 8], P('expert'), may hold values from 0.05 to 0.5
- w_gate: bfloat16 [16, 1024, 4096], P('expert', 'edata'), may hold values from -0.09375 to 0.09375
- w_up: bfloat16 [16, 1024, 4096], P('expert', 'edata'), may hold values from -0.09375 to 0.09375
- w_down: bfloat16 [16, 1024, 4096], P('expert', 'edata'), may hold values from -0.1875 to 0.1875
Outputs:
- grad_tokens: bfloat16 [1024, 4096], P('expert', 'edata')
- grad_gate: bfloat16 [16, 1024, 4096], P('expert', 'edata')
- grad_up: bfloat16 [16, 1024, 4096], P('expert', 'edata')
- grad_down: bfloat16 [16, 1024, 4096], P('expert', 'edata')
Inputs may be any that keep to these rules, and one draw needn't show every extreme that they name: `expert_ids`: each token names 8 different experts. Among the tokens of one aligned block of 128 no expert is named more than 80 times, and in every draw some expert is named exactly 80 times in some block.
All inputs are finite; a program needn't handle non-finite values.
Results may differ from a plain program's by a relative error of at most 0.012.
Values may be sent and summed in bfloat16 or wider, within the bound.
A program may use at most 192 MiB of HBM per device.

v0:
```python
import jax
import jax.numpy as jnp
from jax import lax
from jax.sharding import PartitionSpec as P


def ranks(onehot):
    pair_count = onehot.shape[-2]
    row = lax.broadcasted_iota(jnp.int32, (pair_count, pair_count), 0)
    col = lax.broadcasted_iota(jnp.int32, (pair_count, pair_count), 1)
    tri = (col < row).astype(jnp.bfloat16)
    earlier = jnp.einsum(
        "pq,...qe->...pe", tri, onehot.astype(jnp.bfloat16), preferred_element_type=jnp.float32
    )
    return earlier.astype(jnp.int32)


def body(tokens, grad_out, expert_ids, route_prob, w_gate, w_up, w_down):
    token_count, top_count = expert_ids.shape
    local_experts = w_gate.shape[0]
    expert_devices = lax.axis_size("expert")
    me = lax.axis_index("expert")
    experts_all = expert_devices * local_experts
    capacity = token_count * top_count * 5 // (4 * experts_all)
    pair_count = token_count * top_count
    cap_iota = jnp.arange(capacity, dtype=jnp.int32)
    routing = jnp.stack([expert_ids.astype(jnp.float32), route_prob])
    routing = lax.all_gather(routing, "expert", axis=1, tiled=False)
    all_ids, all_prob = (routing[0].astype(jnp.int32), routing[1])
    mine = me * local_experts + jnp.arange(local_experts, dtype=jnp.int32)
    named = all_ids.reshape(expert_devices, pair_count)[:, :, None] == mine
    rank = ranks(named)
    hit = named[..., None] & (rank[..., None] == cap_iota)
    hit = hit.reshape(expert_devices, token_count, top_count, local_experts, capacity)
    pick = jnp.sum(hit.astype(jnp.int32), 2).astype(jnp.bfloat16)
    prob_of = jnp.sum(jnp.where(hit, all_prob[:, :, :, None, None], 0.0), (1, 2))
    both = lax.all_gather(jnp.stack([tokens, grad_out]), "edata", axis=2, tiled=True)
    both = lax.all_gather(both, "expert", axis=1, tiled=False)
    all_x, all_dy = (both[0], both[1])
    slot_x = jnp.einsum("stxc,std->sxcd", pick, all_x, preferred_element_type=jnp.float32).astype(
        jnp.bfloat16
    )
    slot_dy = jnp.einsum("stxc,std->sxcd", pick, all_dy, preferred_element_type=jnp.float32)
    slot_dy = (prob_of[..., None] * slot_dy).astype(jnp.bfloat16)
    gate_value = jnp.einsum("sxcd,xfd->sxcf", slot_x, w_gate, preferred_element_type=jnp.float32)
    up_value = jnp.einsum("sxcd,xfd->sxcf", slot_x, w_up, preferred_element_type=jnp.float32)
    sigma = jax.nn.sigmoid(gate_value)
    active = gate_value * sigma
    hidden = (active * up_value).astype(jnp.bfloat16)
    back = jnp.einsum("sxcd,xfd->sxcf", slot_dy, w_down, preferred_element_type=jnp.float32)
    gate_grad = (back * up_value * sigma * (1.0 + gate_value * (1.0 - sigma))).astype(jnp.bfloat16)
    up_grad = (back * active).astype(jnp.bfloat16)
    grad_gate = jnp.einsum(
        "sxcf,sxcd->xfd", gate_grad, slot_x, preferred_element_type=jnp.float32
    ).astype(jnp.bfloat16)
    grad_up = jnp.einsum(
        "sxcf,sxcd->xfd", up_grad, slot_x, preferred_element_type=jnp.float32
    ).astype(jnp.bfloat16)
    grad_down = jnp.einsum(
        "sxcf,sxcd->xfd", hidden, slot_dy, preferred_element_type=jnp.float32
    ).astype(jnp.bfloat16)
    partial_value = jnp.einsum(
        "sxcf,xfd->sxcd", gate_grad, w_gate, preferred_element_type=jnp.float32
    )
    partial_value = partial_value + jnp.einsum(
        "sxcf,xfd->sxcd", up_grad, w_up, preferred_element_type=jnp.float32
    )
    partial_value = partial_value.astype(jnp.bfloat16)
    returned = lax.all_to_all(
        partial_value.reshape(expert_devices, local_experts * capacity, -1),
        "expert",
        split_axis=0,
        concat_axis=0,
        tiled=True,
    )
    width = returned.shape[-1]
    own = expert_ids.reshape(pair_count, 1) == jnp.arange(experts_all, dtype=jnp.int32)
    slot = jnp.sum(jnp.where(own, ranks(own), 0), 1)
    back_hit = own[:, :, None] & (slot[:, None, None] == cap_iota)
    gather_back = jnp.sum(
        back_hit.reshape(token_count, top_count, experts_all * capacity).astype(jnp.int32), 1
    ).astype(jnp.bfloat16)
    per_token = jnp.einsum(
        "tq,qd->td",
        gather_back,
        returned.reshape(experts_all * capacity, width),
        preferred_element_type=jnp.float32,
    )
    grad_tokens = lax.psum_scatter(per_token, "edata", scatter_dimension=1, tiled=True).astype(
        jnp.bfloat16
    )
    return (grad_tokens, grad_gate, grad_up, grad_down)


def solution(mesh):
    placed = (
        P("expert", "edata"),
        P("expert", "edata"),
        P("expert", None),
        P("expert", None),
        P("expert", "edata", None),
        P("expert", "edata", None),
        P("expert", "edata", None),
    )
    return jax.shard_map(
        body,
        mesh=mesh,
        in_specs=placed,
        out_specs=(
            P("expert", "edata"),
            P("expert", "edata", None),
            P("expert", "edata", None),
            P("expert", "edata", None),
        ),
        check_vma=False,
    )
```

profile of v0, /device:TPU:0, one launch (start us, length us, event | category | flops | bytes accessed | tf_op | source)
XLA Modules:
  0.0 408.3 jit_solution(9152429621475397026)
XLA Ops:
  7.2 1.9 pad_maximum_fusion
  9.2 49.4 %all-gather.5.cloned.1.call-done = bf16[2,128,4096]{2,1,0:T(8,128)(2,1)} async-done(((bf16[2,128,1024]{2,1,0:T(8,128)(2,1)}), bf16[2,128,4096]{2,1,0:T(8,128)(2,1)}) %all-gather.5.cloned.1.call-update) | async-done | bytes 2097168 | tf_op jit(solution)/shard_map/all_gather | solution.py:37
  59.9 9.0 %all-gather = f32[2,1024,8]{1,2,0:T(8,128)S(1)} all-gather(f32[2,128,8]{1,2,0:T(8,128)S(1)} %pad_maximum_fusion.1), channel_id=2, replica_groups=mesh['edata'=4,'expert'=8] {'expert'}, dimensions={1}, use_global_device_ids=true | all-gather | bytes 73728 | tf_op jit(solution)/shard_map/all_gather | solution.py:28
  73.7 75.3 %all-gather.7.cloned.1.call-done = bf16[2,1024,4096]{2,1,0:T(8,128)(2,1)} async-done(((bf16[2,128,4096]{2,1,0:T(8,128)(2,1)}), bf16[2,1024,4096]{2,1,0:T(8,128)(2,1)}) %all-gather.7.cloned.1.call-update) | async-done | bytes 16777232 | tf_op jit(solution)/shard_map/all_gather | solution.py:38
  149.0 9.5 %fusion.65 = (bf16[1,1024,4096]{2,1,0:T(8,128)(2,1)}, bf16[1,1024,4096]{2,1,0:T(8,128)(2,1)S(1)}) fusion(bf16[2,1024,4096]{2,1,0:T(8,128)(2,1)} %all-gather.7.cloned.1.call-done), kind=kLoop, calls=%fused_computation.65 | loop fusion | bytes 33554432 | tf_op jit(solution)/shard_map/slice | solution.py:39
  158.5 5.5 %convolution_convert_fusion = bf16[8,2,80,4096]{3,2,1,0:T(8,128)(2,1)} fusion(bf16[8,128,4096,1]{2,1,3,0:T(8,128)(2,1)S(1)} %bitcast.84, s32[8,128,2,80]{1,3,2,0:T(8,128)S(1)} %convert_reduce_fusion), kind=kOutput, calls=%fused_computation.11 | convolution fusion | flops 1347584000 | bytes 19529728 | tf_op jit(solution)/shard_map/stxc,std->sxcd/dot_general | solution.py:40
  163.9 9.3 %fusion.35 = f32[8,2,80,256]{3,2,0,1:T(8,128)} fusion(bf16[2,256,4096]{2,1,0:T(8,128)(2,1)} %param.11, bf16[8,2,80,4096]{3,2,1,0:T(8,128)(2,1)} %convolution_convert_fusion), kind=kOutput, calls=%fused_computation.35 | convolution fusion | flops 2684354560 | bytes 15990784 | tf_op jit(solution)/shard_map/sxcd,xfd->sxcf/dot_general | solution.py:45
  173.2 9.3 %fusion.30 = f32[8,2,80,256]{3,2,0,1:T(8,128)} fusion(bf16[2,256,4096]{2,1,0:T(8,128)(2,1)} %param.12, bf16[8,2,80,4096]{3,2,1,0:T(8,128)(2,1)} %convolution_convert_fusion), kind=kOutput, calls=%fused_computation.34 | convolution fusion | flops 2684354560 | bytes 15990784 | tf_op jit(solution)/shard_map/sxcd,xfd->sxcf/dot_general | solution.py:46
  182.5 5.4 %multiply_convert_fusion = bf16[8,2,80,4096]{3,2,1,0:T(8,128)(2,1)} fusion(f32[8,2,80]{2,1,0:T(2,128)S(1)} %select_reduce_fusion, bf16[8,128,4096,1]{2,1,3,0:T(8,128)(2,1)S(1)} %bitcast.87, s32[8,128,2,80]{1,3,2,0:T(8,128)S(1)} %convert_reduce_fusion), kind=kOutput, calls=%fused_computation.1 | convolution fusion | flops 1352826880 | bytes 19534848 | tf_op jit(solution)/shard_map/stxc,std->sxcd/dot_general | solution.py:43
  187.9 9.4 %multiply_convert_fusion.2 = (bf16[8,2,80,256]{3,2,0,1:T(8,128)(2,1)S(1)}, bf16[8,2,80,256]{3,2,0,1:T(8,128)(2,1)S(1)}) fusion(f32[8,2,80,256]{3,2,0,1:T(8,128)} %fusion.35, f32[8,2,80,256]{3,2,0,1:T(8,128)} %fusion.30, bf16[2,256,4096]{2,1,0:T(8,128)(2,1)} %param.13, bf16[8,2,80,4096]{3,2,1,0:T(8,128)(2,1)} %multiply_convert_fusion), kind=kOutput, calls=%fused_computation.38 | convolution fusion | flops 2688614400 | bytes 18612224 | tf_op jit(solution)/shard_map/sxcd,xfd->sxcf/dot_general | solution.py:50
  197.3 8.7 %fusion.20 = f32[2,8,80,4096]{3,2,1,0:T(8,128)} fusion(bf16[8,2,80,256]{3,2,0,1:T(8,128)(2,1)S(1)} %get-tuple-element.7, bf16[2,256,4096]{2,1,0:T(8,128)(2,1)S(1)} %copy-done), kind=kOutput, calls=%fused_computation.24 | convolution fusion | flops 2684354560 | bytes 25821184 | tf_op jit(solution)/shard_map/sxcf,xfd->sxcd/dot_general | solution.py:62
  206.0 13.0 %fusion = bf16[8,2,80,4096]{3,2,0,1:T(8,128)(2,1)} fusion(f32[2,8,80,4096]{3,2,1,0:T(8,128)} %fusion.20, bf16[8,2,80,256]{3,2,0,1:T(8,128)(2,1)S(1)} %get-tuple-element.6, bf16[2,256,4096]{2,1,0:T(8,128)(2,1)} %param.12), kind=kOutput, calls=%fused_computation.2 | convolution fusion | flops 2694840320 | bytes 36306944 | tf_op jit(solution)/shard_map/sxcf,xfd->sxcd/dot_general | solution.py:65
  219.0 9.4 %copy.42 = bf16[8,2,80,4096]{3,2,1,0:T(8,128)(2,1)} copy(bf16[8,2,80,4096]{3,2,0,1:T(8,128)(2,1)} %fusion) | data formatting | bytes 20971520 | tf_op jit(solution)/shard_map/convert_element_type | solution.py:68
  228.4 5.3 %all-to-all-start = ((bf16[8,160,4096]{2,1,0:T(8,128)(2,1)}), bf16[8,160,4096]{2,1,0:T(8,128)(2,1)}, u32[]{:S(2)}, u32[]{:S(2)}) async-start(bf16[8,160,4096]{2,1,0:T(8,128)(2,1)} %bitcast.83), calls=%async_computation | async-start | bytes 20971520 | tf_op jit(solution)/shard_map/all_to_all | solution.py:69
  235.0 7.9 %and_convert_fusion = s32[1024,16,80]{2,1,0:T(8,128)} fusion(pred[1024,80]{1,0:T(8,128)(4,1)S(1)} %iota_compare_fusion.9, pred[1024,16]{1,0:T(8,128)(4,1)S(1)} %copy.35), kind=kLoop, calls=%fused_computation.10 | loop fusion | flops 2621440 | bytes 5341184 | tf_op jit(solution)/shard_map/convert_element_type | solution.py:81
  242.8 9.1 %reshape.90 = s32[128,8,1280]{2,1,0:T(8,128)} reshape(s32[1024,16,80]{2,1,0:T(8,128)} %and_convert_fusion) | data formatting | bytes 10485760 | tf_op jit(solution)/shard_map/convert_element_type | solution.py:81
  251.9 3.7 reduce_sum.37
  255.7 94.6 %all-to-all-done = bf16[8,160,4096]{2,1,0:T(8,128)(2,1)} async-done(((bf16[8,160,4096]{2,1,0:T(8,128)(2,1)}), bf16[8,160,4096]{2,1,0:T(8,128)(2,1)}, u32[]{:S(2)}, u32[]{:S(2)}) %all-to-all-start) | async-done | bytes 10485792 | tf_op jit(solution)/shard_map/all_to_all | solution.py:69
  350.2 6.8 %fusion.55 = f32[128,4096]{1,0:T(8,128)} fusion(bf16[1280,4096]{1,0:T(8,128)(2,1)} %bitcast.26, s32[128,1280]{1,0:T(8,128)S(1)} %reduce_sum.37), kind=kOutput, calls=%fused_computation.49 | convolution fusion | flops 1342341120 | bytes 13238272 | tf_op jit(solution)/shard_map/tq,qd->td/dot_general | solution.py:83
  357.1 9.2 %bitcast_convert_fusion.1 = bf16[2,256,4096]{2,1,0:T(8,128)(2,1)} fusion(bf16[8,2,80,256]{3,2,0,1:T(8,128)(2,1)S(1)} %get-tuple-element.6, bf16[8,2,80,4096]{3,2,1,0:T(8,128)(2,1)} %convolution_convert_fusion), kind=kOutput, calls=%fused_computation.8 | convolution fusion | flops 2686451712 | bytes 15335424 | tf_op jit(solution)/shard_map/sxcf,sxcd->xfd/dot_general | solution.py:56
  366.3 9.3 %bitcast_convert_fusion.2 = bf16[2,256,4096]{2,1,0:T(8,128)(2,1)} fusion(bf16[8,2,80,256]{3,2,0,1:T(8,128)(2,1)S(1)} %get-tuple-element.7, bf16[8,2,80,4096]{3,2,1,0:T(8,128)(2,1)} %convolution_convert_fusion), kind=kOutput, calls=%fused_computation.9 | convolution fusion | flops 2686451712 | bytes 15335424 | tf_op jit(solution)/shard_map/sxcf,sxcd->xfd/dot_general | solution.py:53
  375.6 5.3 %bitcast_convert_fusion = bf16[2,256,4096]{2,1,0:T(8,128)(2,1)} fusion(bf16[8,2,80,4096]{3,2,1,0:T(8,128)(2,1)S(1)} %bitcast.89, f32[8,2,80,256]{3,2,0,1:T(8,128)S(1)} %copy-done.3, f32[8,2,80,256]{3,2,0,1:T(8,128)S(1)} %copy-done.2), kind=kOutput, calls=%fused_computation.7 | convolution fusion | flops 2688417792 | bytes 17301504 | tf_op jit(solution)/shard_map/sxcf,sxcd->xfd/dot_general | solution.py:59
  381.0 19.0 %reduce-scatter.2.cloned.1.call-done = f32[128,1024]{1,0:T(8,128)} async-done(((f32[128,4096]{1,0:T(8,128)}), f32[128,1024]{1,0:T(8,128)}) %reduce-scatter.2.cloned.1.call-update) | async-done | bytes 524304 | tf_op jit(solution)/shard_map/reduce_scatter | solution.py:89
  400.0 1.8 convert_element_type.96
  (45 shorter events, 7.4 us)
Async XLA Ops:
  7.2 51.4 %all-gather.5.cloned.1.call-start = ((), (), s32[]{:S(2)}) async-start(), calls=%async_computation.2 | async-start | bytes 2621440 | tf_op jit(solution)/shard_map/all_gather | solution.py:37
  9.1 139.9 %all-gather.7.cloned.1.call-start = ((), (), s32[]{:S(2)}) async-start(), calls=%async_computation.4 | async-start | bytes 18874368 | tf_op jit(solution)/shard_map/all_gather | solution.py:38
  163.9 18.6 %slice-start = ((s8[8388608]{0:T(1024)(128)(4,1)}), s8[4194304]{0:T(1024)(128)(4,1)S(1)}, s32[]{:S(2)}) async-start(s8[8388608]{0:T(1024)(128)(4,1)} %bitcast.85), calls=%async_computation.5 | async-start | bytes 8388608
  173.2 9.3 %slice-start.1 = ((s8[8388608]{0:T(1024)(128)(4,1)}), s8[4194304]{0:T(1024)(128)(4,1)S(1)}, s32[]{:S(2)}) async-start(s8[8388608]{0:T(1024)(128)(4,1)} %bitcast.85), calls=%async_computation.6 | async-start | bytes 8388608
  187.9 9.4 %copy-start = (bf16[2,256,4096]{2,1,0:T(8,128)(2,1)S(1)}, bf16[2,256,4096]{2,1,0:T(8,128)(2,1)}, u32[]{:S(2)}) copy-start(bf16[2,256,4096]{2,1,0:T(8,128)(2,1)} %param.11) | copy-start | bytes 12582916
  228.4 5.4 %copy-start.1 = (s32[128,8]{0,1:T(8,128)S(1)}, s32[128,8]{0,1:T(8,128)}, u32[]{:S(2)}) copy-start(s32[128,8]{0,1:T(8,128)} %param.9) | copy-start | bytes 12292
  228.4 121.8 %all-to-all-start = ((bf16[8,160,4096]{2,1,0:T(8,128)(2,1)}), bf16[8,160,4096]{2,1,0:T(8,128)(2,1)}, u32[]{:S(2)}, u32[]{:S(2)}) async-start(bf16[8,160,4096]{2,1,0:T(8,128)(2,1)} %bitcast.83), calls=%async_computation | async-start | bytes 20971520 | tf_op jit(solution)/shard_map/all_to_all | solution.py:69
  233.7 166.3 %reduce-scatter.2.cloned.1.call-start = ((), (), s32[]{:S(2)}) async-start(), calls=%async_computation.3 | async-start | bytes 2621440 | tf_op jit(solution)/shard_map/reduce_scatter | solution.py:89
  357.1 18.5 %slice-start.2 = ((s8[10485760]{0:T(1024)(128)(4,1)}), s8[4194304]{0:T(1024)(128)(4,1)S(1)}, s32[]{:S(2)}) async-start(s8[10485760]{0:T(1024)(128)(4,1)} %bitcast.88), calls=%async_computation.7 | async-start | bytes 8388608
  357.1 18.5 %slice-start.3 = ((s8[10485760]{0:T(1024)(128)(4,1)}), s8[4194304]{0:T(1024)(128)(4,1)S(1)}, s32[]{:S(2)}) async-start(s8[10485760]{0:T(1024)(128)(4,1)} %bitcast.88), calls=%async_computation.8 | async-start | bytes 8388608
  366.3 9.3 %slice-start.4 = ((s8[10485760]{0:T(1024)(128)(4,1)}), s8[2097152]{0:T(1024)(128)(4,1)S(1)}, s32[]{:S(2)}) async-start(s8[10485760]{0:T(1024)(128)(4,1)} %bitcast.88), calls=%async_computation.9 | async-start | bytes 4194304
  366.3 9.3 %copy-start.2 = (f32[8,2,80,256]{3,2,0,1:T(8,128)S(1)}, f32[8,2,80,256]{3,2,0,1:T(8,128)}, u32[]{:S(2)}) copy-start(f32[8,2,80,256]{3,2,0,1:T(8,128)} %fusion.35) | copy-start | bytes 3932164
  366.3 9.3 %copy-start.3 = (f32[8,2,80,256]{3,2,0,1:T(8,128)S(1)}, f32[8,2,80,256]{3,2,0,1:T(8,128)}, u32[]{:S(2)}) copy-start(f32[8,2,80,256]{3,2,0,1:T(8,128)} %fusion.30) | copy-start | bytes 3932164
Sparse Core Ops, SparseCore 0:
  10.1 48.3 all-gather.4
  60.4 88.5 all-gather.6
  357.2 42.7 reduce-scatter.1
where the time goes:
time: 409 us; the launch traced here: 408 us
  waiting for transfers between devices  238 us (58%)
  matrix products  92.1 us (23%)
  local copies, waits for them, and re-layouts  29.9 us (7%)
  other arithmetic  19.5 us (5%)
  between operations  13.9 us (3%)
  blocking collectives  9.03 us (2%)
  starting transfers between devices  5.41 us (1%)
    all_to_all x1, waiting for transfers between devices, body(): lax.all_to_all(partial_value.reshape(expert_devices, local_experts * capa...  94.6 us
    all_gather x1, waiting for transfers between devices, body(): both = lax.all_gather(both, 'expert', axis=1, tiled=False)  75.3 us
    all_gather x1, waiting for transfers between devices, body(): lax.all_gather(jnp.stack([tokens, grad_out]), 'edata', axis=2, tiled=True)  49.4 us
    reduce_scatter x1, waiting for transfers between devices, body(): lax.psum_scatter(per_token, 'edata', scatter_dimension=1, tiled=True)  19 us
    dot_general x1, matrix products, body(): jnp.einsum('sxcf,xfd->sxcd', up_grad, w_up, preferred_element_type=jnp.fl...  13 us
    slice x1, local copies, waits for them, and re-layouts, body(): all_x, all_dy = (both[0], both[1])  9.49 us
    convert_element_type x1, local copies, waits for them, and re-layouts, body(): partial_value = partial_value.astype(jnp.bfloat16)  9.44 us
    dot_general x1, matrix products, body(): jnp.einsum('sxcd,xfd->sxcf', slot_dy, w_down, preferred_element_type=jnp....  9.36 us
  transfers between devices with their start and end apart: 4, of which 4 were waited for; matrix products, arithmetic and copies ran while one was open for 13% of the time, Pallas kernels for 0%

commit v1 on v0

--- a/solution.py
+++ b/solution.py
@@ -2,6 +2,27 @@
 import jax.numpy as jnp
 from jax import lax
 from jax.sharding import PartitionSpec as P
+
+
+def ring_gather(array, axis, dim):
+    peers, index, span = (lax.axis_size(axis), lax.axis_index(axis), array.shape[dim])
+    ahead = [(i, (i + 1) % peers) for i in range(peers)]
+    left = [(i, (i - 1) % peers) for i in range(peers)]
+    result = jnp.zeros((*array.shape[:dim], peers * span, *array.shape[dim + 1 :]), array.dtype)
+    result = lax.dynamic_update_slice_in_dim(result, array, index * span, axis=dim)
+    from_left = from_right = array
+    half = peers // 2
+    for lap in range(1, half + 1):
+        from_left = lax.ppermute(from_left, axis, ahead)
+        result = lax.dynamic_update_slice_in_dim(
+            result, from_left, (index - lap) % peers * span, axis=dim
+        )
+        if lap < peers - half:
+            from_right = lax.ppermute(from_right, axis, left)
+            result = lax.dynamic_update_slice_in_dim(
+                result, from_right, (index + lap) % peers * span, axis=dim
+            )
+    return result
 
 
 def ranks(onehot):
@@ -34,7 +55,7 @@
     hit = hit.reshape(expert_devices, token_count, top_count, local_experts, capacity)
     pick = jnp.sum(hit.astype(jnp.int32), 2).astype(jnp.bfloat16)
     prob_of = jnp.sum(jnp.where(hit, all_prob[:, :, :, None, None], 0.0), (1, 2))
-    both = lax.all_gather(jnp.stack([tokens, grad_out]), "edata", axis=2, tiled=True)
+    both = ring_gather(jnp.stack([tokens, grad_out]), "edata", 2)
     both = lax.all_gather(both, "expert", axis=1, tiled=False)
     all_x, all_dy = (both[0], both[1])
     slot_x = jnp.einsum("stxc,std->sxcd", pick, all_x, preferred_element_type=jnp.float32).astype(

time: 409 us -> 395 us (0.966)
  waiting for transfers between devices: 238 us -> 221 us
  local copies, waits for them, and re-layouts: 29.9 us -> 24.2 us
  starting transfers between devices: 5.41 us -> 10.7 us
  matrix products: 92.1 us -> 97.1 us
    all_gather x1 -> x0, waiting for transfers between devices: 49.4 us -> none  [body(): lax.all_gather(jnp.stack([tokens, grad_out]), 'edata', axis=2, tiled=True)]
    ppermute x0 -> x3, waiting for transfers between devices: none -> 32 us  [the longest x2 23.3 us: ring_gather(): from_left = lax.ppermute(from_left, axis, ahead)]
    slice x1 -> x0, local copies, waits for them, and re-layouts: 9.49 us -> none  [body(): all_x, all_dy = (both[0], both[1])]
    ppermute x0 -> x3, starting transfers between devices: none -> 5.2 us  [the longest x2 3.11 us: ring_gather(): from_left = lax.ppermute(from_left, axis, ahead)]
    dot_general x1, matrix products: 5.46 us -> 10.2 us  [body(): jnp.einsum('stxc,std->sxcd', pick, all_x, preferred_element_type=jnp.floa...]
  transfers between devices with their start and end apart: 4 -> 6, of which waited for: 4 -> 6; matrix products, arithmetic and copies ran while one was open for 13% -> 13% of each run, Pallas kernels for 0% -> 0%
where the time goes in v1:
time: 395 us
  waiting for transfers between devices  221 us (56%)
  matrix products  97.1 us (25%)
  local copies, waits for them, and re-layouts  24.2 us (6%)
  other arithmetic  18.5 us (5%)
  between operations  14.3 us (4%)
  starting transfers between devices  10.7 us (3%)
  blocking collectives  9.1 us (2%)
    all_to_all x1, waiting for transfers between devices, body(): lax.all_to_all(partial_value.reshape(expert_devices, local_experts * capa...  94.4 us
    all_gather x1, waiting for transfers between devices, body(): both = lax.all_gather(both, 'expert', axis=1, tiled=False)  75.4 us
    ppermute x2, waiting for transfers between devices, ring_gather(): from_left = lax.ppermute(from_left, axis, ahead)  23.3 us
    reduce_scatter x1, waiting for transfers between devices, body(): lax.psum_scatter(per_token, 'edata', scatter_dimension=1, tiled=True)  19 us
    dot_general x1, matrix products, body(): jnp.einsum('sxcf,xfd->sxcd', up_grad, w_up, preferred_element_type=jnp.fl...  13 us
    dot_general x1, matrix products, body(): jnp.einsum('stxc,std->sxcd', pick, all_x, preferred_element_type=jnp.floa...  10.2 us
    convert_element_type x1, local copies, waits for them, and re-layouts, body(): partial_value = partial_value.astype(jnp.bfloat16)  9.45 us
    dot_general x1, matrix products, body(): jnp.einsum('sxcd,xfd->sxcf', slot_dy, w_down, preferred_element_type=jnp....  9.36 us
  transfers between devices with their start and end apart: 6, of which 6 were waited for; matrix products, arithmetic and copies ran while one was open for 13% of the time, Pallas kernels for 0%

profile of v1, /device:TPU:0, one launch (start us, length us, event | category | flops | bytes accessed | tf_op | source)
XLA Modules:
  0.0 394.6 jit_solution(16731630980664390543)
XLA Ops:
  8.3 3.1 collective-permute-start
  13.5 12.7 %collective-permute-done = bf16[2,128,1024]{2,1,0:T(8,128)(2,1)S(1)} collective-permute-done((bf16[2,128,1024]{2,1,0:T(8,128)(2,1)S(1)}, bf16[2,128,1024]{2,1,0:T(8,128)(2,1)S(1)}, u32[]{:S(2)}, u32[]{:S(2)}) %collective-permute-start) | collective-permute-done | bytes 524320 | tf_op jit(solution)/shard_map/ppermute | solution.py:16
  27.7 8.7 %collective-permute-done.1 = bf16[2,128,1024]{2,1,0:T(8,128)(2,1)} collective-permute-done((bf16[2,128,1024]{2,1,0:T(8,128)(2,1)S(1)}, bf16[2,128,1024]{2,1,0:T(8,128)(2,1)}, u32[]{:S(2)}, u32[]{:S(2)}) %collective-permute-start.1) | collective-permute-done | bytes 524320 | tf_op jit(solution)/shard_map/ppermute | solution.py:21
  37.4 10.5 %collective-permute-done.2 = bf16[2,128,1024]{2,1,0:T(8,128)(2,1)} collective-permute-done((bf16[2,128,1024]{2,1,0:T(8,128)(2,1)S(1)}, bf16[2,128,1024]{2,1,0:T(8,128)(2,1)}, u32[]{:S(2)}, u32[]{:S(2)}) %collective-permute-start.2) | collective-permute-done | bytes 524320 | tf_op jit(solution)/shard_map/ppermute | solution.py:16
  50.4 9.1 %all-gather = f32[2,1024,8]{1,2,0:T(8,128)S(1)} all-gather(f32[2,128,8]{1,2,0:T(8,128)S(1)} %pad_maximum_fusion.1), channel_id=2, replica_groups=mesh['edata'=4,'expert'=8] {'expert'}, dimensions={1}, use_global_device_ids=true | all-gather | bytes 73728 | tf_op jit(solution)/shard_map/all_gather | solution.py:49
  64.2 75.4 %all-gather.3.cloned.1.call-done = bf16[2,8,128,4096]{3,2,1,0:T(8,128)(2,1)} async-done(((bf16[2,1,128,4096]{3,2,1,0:T(8,128)(2,1)}), bf16[2,8,128,4096]{3,2,1,0:T(8,128)(2,1)}) %all-gather.3.cloned.1.call-update) | async-done | bytes 16777232 | tf_op jit(solution)/shard_map/all_gather | solution.py:59
  139.6 10.2 %fusion.7 = bf16[8,2,80,4096]{3,2,1,0:T(8,128)(2,1)} fusion(bf16[2,8,128,4096]{3,2,1,0:T(8,128)(2,1)} %all-gather.3.cloned.1.call-done, s32[8,128,2,80]{1,3,2,0:T(8,128)S(1)} %convert_reduce_fusion), kind=kOutput, calls=%fused_computation.15 | convolution fusion | flops 1347584000 | bytes 19529728 | tf_op jit(solution)/shard_map/stxc,std->sxcd/dot_general | solution.py:61
  149.8 9.3 %fusion.38 = f32[8,2,80,256]{3,2,0,1:T(8,128)} fusion(bf16[2,256,4096]{2,1,0:T(8,128)(2,1)} %param.11, bf16[8,2,80,4096]{3,2,1,0:T(8,128)(2,1)} %fusion.7), kind=kOutput, calls=%fused_computation.39 | convolution fusion | flops 2684354560 | bytes 15990784 | tf_op jit(solution)/shard_map/sxcd,xfd->sxcf/dot_general | solution.py:66
  159.1 6.3 %fusion.33 = f32[8,2,80,256]{3,2,0,1:T(8,128)} fusion(bf16[2,256,4096]{2,1,0:T(8,128)(2,1)} %param.12, bf16[8,2,80,4096]{3,2,1,0:T(8,128)(2,1)S(1)} %copy-done), kind=kOutput, calls=%fused_computation.38 | convolution fusion | flops 2684354560 | bytes 15990784 | tf_op jit(solution)/shard_map/sxcd,xfd->sxcf/dot_general | solution.py:67
  165.5 8.7 %multiply_convert_fusion = bf16[8,2,80,4096]{3,2,1,0:T(8,128)(2,1)} fusion(f32[8,2,80]{2,1,0:T(2,128)S(1)} %select_reduce_fusion, bf16[2,8,128,4096]{3,2,1,0:T(8,128)(2,1)} %all-gather.3.cloned.1.call-done, s32[8,128,2,80]{1,3,2,0:T(8,128)S(1)} %convert_reduce_fusion), kind=kOutput, calls=%fused_computation.1 | convolution fusion | flops 1352826880 | bytes 19534848 | tf_op jit(solution)/shard_map/stxc,std->sxcd/dot_general | solution.py:64
  174.2 9.4 %multiply_convert_fusion.2 = (bf16[8,2,80,256]{3,2,0,1:T(8,128)(2,1)S(1)}, bf16[8,2,80,256]{3,2,0,1:T(8,128)(2,1)S(1)}) fusion(f32[8,2,80,256]{3,2,0,1:T(8,128)} %fusion.38, f32[8,2,80,256]{3,2,0,1:T(8,128)} %fusion.33, bf16[2,256,4096]{2,1,0:T(8,128)(2,1)} %param.13, bf16[8,2,80,4096]{3,2,1,0:T(8,128)(2,1)} %multiply_convert_fusion), kind=kOutput, calls=%fused_computation.42 | convolution fusion | flops 2688614400 | bytes 18612224 | tf_op jit(solution)/shard_map/sxcd,xfd->sxcf/dot_general | solution.py:71
  183.6 8.5 %fusion.23 = f32[2,8,80,4096]{3,2,1,0:T(8,128)} fusion(bf16[8,2,80,256]{3,2,0,1:T(8,128)(2,1)S(1)} %get-tuple-element.5, bf16[2,256,4096]{2,1,0:T(8,128)(2,1)S(1)} %copy-done.2), kind=kOutput, calls=%fused_computation.28 | convolution fusion | flops 2684354560 | bytes 25821184 | tf_op jit(solution)/shard_map/sxcf,xfd->sxcd/dot_general | solution.py:83
  192.1 13.0 %fusion = bf16[8,2,80,4096]{3,2,0,1:T(8,128)(2,1)} fusion(f32[2,8,80,4096]{3,2,1,0:T(8,128)} %fusion.23, bf16[8,2,80,256]{3,2,0,1:T(8,128)(2,1)S(1)} %get-tuple-element.4, bf16[2,256,4096]{2,1,0:T(8,128)(2,1)} %param.12), kind=kOutput, calls=%fused_computation.2 | convolution fusion | flops 2694840320 | bytes 36306944 | tf_op jit(solution)/shard_map/sxcf,xfd->sxcd/dot_general | solution.py:86
  205.1 9.4 %copy.51 = bf16[8,2,80,4096]{3,2,1,0:T(8,128)(2,1)} copy(bf16[8,2,80,4096]{3,2,0,1:T(8,128)(2,1)} %fusion) | data formatting | bytes 20971520 | tf_op jit(solution)/shard_map/convert_element_type | solution.py:89
  214.5 5.2 %all-to-all-start = ((bf16[8,160,4096]{2,1,0:T(8,128)(2,1)}), bf16[8,160,4096]{2,1,0:T(8,128)(2,1)}, u32[]{:S(2)}, u32[]{:S(2)}) async-start(bf16[8,160,4096]{2,1,0:T(8,128)(2,1)} %bitcast.101), calls=%async_computation | async-start | bytes 20971520 | tf_op jit(solution)/shard_map/all_to_all | solution.py:90
  221.2 7.9 %and_convert_fusion = s32[1024,16,80]{2,1,0:T(8,128)} fusion(pred[1024,80]{1,0:T(8,128)(4,1)S(1)} %iota_compare_fusion.9, pred[1024,16]{1,0:T(8,128)(4,1)S(1)} %copy.41), kind=kLoop, calls=%fused_computation.14 | loop fusion | flops 2621440 | bytes 5341184 | tf_op jit(solution)/shard_map/convert_element_type | solution.py:102
  229.1 9.1 %reshape.98 = s32[128,8,1280]{2,1,0:T(8,128)} reshape(s32[1024,16,80]{2,1,0:T(8,128)} %and_convert_fusion) | data formatting | bytes 10485760 | tf_op jit(solution)/shard_map/convert_element_type | solution.py:102
  238.1 3.7 reduce_sum.37
  241.9 94.4 %all-to-all-done = bf16[8,160,4096]{2,1,0:T(8,128)(2,1)} async-done(((bf16[8,160,4096]{2,1,0:T(8,128)(2,1)}), bf16[8,160,4096]{2,1,0:T(8,128)(2,1)}, u32[]{:S(2)}, u32[]{:S(2)}) %all-to-all-start) | async-done | bytes 10485792 | tf_op jit(solution)/shard_map/all_to_all | solution.py:90
  336.2 6.8 %fusion.58 = f32[128,4096]{1,0:T(8,128)} fusion(bf16[1280,4096]{1,0:T(8,128)(2,1)} %bitcast.33, s32[128,1280]{1,0:T(8,128)S(1)} %reduce_sum.37), kind=kOutput, calls=%fused_computation.57 | convolution fusion | flops 1342341120 | bytes 13238272 | tf_op jit(solution)/shard_map/tq,qd->td/dot_general | solution.py:104
  343.1 9.2 %bitcast_convert_fusion.1 = bf16[2,256,4096]{2,1,0:T(8,128)(2,1)} fusion(bf16[8,2,80,256]{3,2,0,1:T(8,128)(2,1)S(1)} %get-tuple-element.4, bf16[8,2,80,4096]{3,2,1,0:T(8,128)(2,1)} %fusion.7), kind=kOutput, calls=%fused_computation.12 | convolution fusion | flops 2686451712 | bytes 15335424 | tf_op jit(solution)/shard_map/sxcf,sxcd->xfd/dot_general | solution.py:77
  352.3 9.3 %bitcast_convert_fusion.2 = bf16[2,256,4096]{2,1,0:T(8,128)(2,1)} fusion(bf16[8,2,80,256]{3,2,0,1:T(8,128)(2,1)S(1)} %get-tuple-element.5, bf16[8,2,80,4096]{3,2,1,0:T(8,128)(2,1)} %fusion.7), kind=kOutput, calls=%fused_computation.13 | convolution fusion | flops 2686451712 | bytes 15335424 | tf_op jit(solution)/shard_map/sxcf,sxcd->xfd/dot_general | solution.py:74
  361.6 5.3 %bitcast_convert_fusion = bf16[2,256,4096]{2,1,0:T(8,128)(2,1)} fusion(bf16[8,2,80,4096]{3,2,1,0:T(8,128)(2,1)S(1)} %bitcast.103, f32[8,2,80,256]{3,2,0,1:T(8,128)S(1)} %copy-done.6, f32[8,2,80,256]{3,2,0,1:T(8,128)S(1)} %copy-done.5), kind=kOutput, calls=%fused_computation.11 | convolution fusion | flops 2688417792 | bytes 17301504 | tf_op jit(solution)/shard_map/sxcf,sxcd->xfd/dot_general | solution.py:80
  367.0 19.0 %reduce-scatter.2.cloned.1.call-done = f32[128,1024]{1,0:T(8,128)} async-done(((f32[128,4096]{1,0:T(8,128)}), f32[128,1024]{1,0:T(8,128)}) %reduce-scatter.2.cloned.1.call-update) | async-done | bytes 524304 | tf_op jit(solution)/shard_map/reduce_scatter | solution.py:110
  (53 shorter events, 15.9 us)
Async XLA Ops:
  7.2 132.5 %all-gather.3.cloned.1.call-start = ((), (), s32[]{:S(2)}) async-start(), calls=%async_computation.2 | async-start | bytes 18874368 | tf_op jit(solution)/shard_map/all_gather | solution.py:59
  8.3 17.9 %collective-permute-start = (bf16[2,128,1024]{2,1,0:T(8,128)(2,1)S(1)}, bf16[2,128,1024]{2,1,0:T(8,128)(2,1)S(1)}, u32[]{:S(2)}, u32[]{:S(2)}) collective-permute-start(bf16[2,128,1024]{2,1,0:T(8,128)(2,1)S(1)} %pad_maximum_fusion), channel_id=1, source_target_pairs={{0,8},{8,16},{16,24},{24,0},{1,9},{9,17},{17,25},{25,1},{2,10},{10... | collective-permute-start | bytes 1572872 | tf_op jit(solution)/shard_map/ppermute | solution.py:16
  11.4 25.0 %collective-permute-start.1 = (bf16[2,128,1024]{2,1,0:T(8,128)(2,1)S(1)}, bf16[2,128,1024]{2,1,0:T(8,128)(2,1)}, u32[]{:S(2)}, u32[]{:S(2)}) collective-permute-start(bf16[2,128,1024]{2,1,0:T(8,128)(2,1)S(1)} %pad_maximum_fusion), channel_id=1, source_target_pairs={{0,24},{8,0},{16,8},{24,16},{1,25},{9,1},{17,9},{25,17},{2,26},{10... | collective-permute-start | bytes 1572872 | tf_op jit(solution)/shard_map/ppermute | solution.py:21
  13.5 36.9 %copy-start.3 = (s32[128,8]{0,1:T(8,128)S(1)}, s32[128,8]{0,1:T(8,128)}, u32[]{:S(2)}) copy-start(s32[128,8]{0,1:T(8,128)} %param.9) | copy-start | bytes 12292
  13.5 36.9 %copy-start.4 = (f32[128,8]{0,1:T(8,128)S(1)}, f32[128,8]{0,1:T(8,128)}, u32[]{:S(2)}) copy-start(f32[128,8]{0,1:T(8,128)} %param.10) | copy-start | bytes 12292
  26.2 21.7 %collective-permute-start.2 = (bf16[2,128,1024]{2,1,0:T(8,128)(2,1)S(1)}, bf16[2,128,1024]{2,1,0:T(8,128)(2,1)}, u32[]{:S(2)}, u32[]{:S(2)}) collective-permute-start(bf16[2,128,1024]{2,1,0:T(8,128)(2,1)S(1)} %collective-permute-done), channel_id=1, source_target_pairs={{0,8},{8,16},{16,24},{24,0},{1,9},{9,17},{17,25},{25,1},{2,10},{10... | collective-permute-start | bytes 1572872 | tf_op jit(solution)/shard_map/ppermute | solution.py:16
  49.1 1.3 copy-start.1
  149.8 9.3 %copy-start = (bf16[8,2,80,4096]{3,2,1,0:T(8,128)(2,1)S(1)}, bf16[8,2,80,4096]{3,2,1,0:T(8,128)(2,1)}, u32[]{:S(2)}) copy-start(bf16[8,2,80,4096]{3,2,1,0:T(8,128)(2,1)} %fusion.7) | copy-start | bytes 31457284
  174.2 9.4 %copy-start.2 = (bf16[2,256,4096]{2,1,0:T(8,128)(2,1)S(1)}, bf16[2,256,4096]{2,1,0:T(8,128)(2,1)}, u32[]{:S(2)}) copy-start(bf16[2,256,4096]{2,1,0:T(8,128)(2,1)} %param.11) | copy-start | bytes 12582916
  214.5 121.7 %all-to-all-start = ((bf16[8,160,4096]{2,1,0:T(8,128)(2,1)}), bf16[8,160,4096]{2,1,0:T(8,128)(2,1)}, u32[]{:S(2)}, u32[]{:S(2)}) async-start(bf16[8,160,4096]{2,1,0:T(8,128)(2,1)} %bitcast.101), calls=%async_computation | async-start | bytes 20971520 | tf_op jit(solution)/shard_map/all_to_all | solution.py:90
  219.7 166.3 %reduce-scatter.2.cloned.1.call-start = ((), (), s32[]{:S(2)}) async-start(), calls=%async_computation.3 | async-start | bytes 2621440 | tf_op jit(solution)/shard_map/reduce_scatter | solution.py:110
  343.1 18.5 %slice-start = ((s8[10485760]{0:T(1024)(128)(4,1)}), s8[4194304]{0:T(1024)(128)(4,1)S(1)}, s32[]{:S(2)}) async-start(s8[10485760]{0:T(1024)(128)(4,1)} %bitcast.102), calls=%async_computation.4 | async-start | bytes 8388608
  343.1 18.5 %slice-start.1 = ((s8[10485760]{0:T(1024)(128)(4,1)}), s8[4194304]{0:T(1024)(128)(4,1)S(1)}, s32[]{:S(2)}) async-start(s8[10485760]{0:T(1024)(128)(4,1)} %bitcast.102), calls=%async_computation.5 | async-start | bytes 8388608
  352.3 9.3 %slice-start.2 = ((s8[10485760]{0:T(1024)(128)(4,1)}), s8[2097152]{0:T(1024)(128)(4,1)S(1)}, s32[]{:S(2)}) async-start(s8[10485760]{0:T(1024)(128)(4,1)} %bitcast.102), calls=%async_computation.6 | async-start | bytes 4194304
  352.3 9.3 %copy-start.5 = (f32[8,2,80,256]{3,2,0,1:T(8,128)S(1)}, f32[8,2,80,256]{3,2,0,1:T(8,128)}, u32[]{:S(2)}) copy-start(f32[8,2,80,256]{3,2,0,1:T(8,128)} %fusion.38) | copy-start | bytes 3932164
  352.3 9.3 %copy-start.6 = (f32[8,2,80,256]{3,2,0,1:T(8,128)S(1)}, f32[8,2,80,256]{3,2,0,1:T(8,128)}, u32[]{:S(2)}) copy-start(f32[8,2,80,256]{3,2,0,1:T(8,128)} %fusion.33) | copy-start | bytes 3932164
Sparse Core Ops, SparseCore 0:
  50.5 89.0 all-gather.2
  343.2 42.7 reduce-scatter.1
